TPU v7x, 32 devices: a whole 2x2x4 slice. The times are simulated.
32 devices in a mesh: tok: 8 (over z, core), voc: 4 (over y, x).
Axes of the slice: x: 2, y: 2, z: 4, core: 2. Of those that a mesh axis runs over, the one named last changes fastest.
Arguments:
- hidden: bfloat16 [4096, 1024], P('tok'), may hold values from -64 to 64
- head_weight: bfloat16 [1024, 16384], P('tok', 'voc'), may hold values from -1 to 1
- target_logits: bfloat16 [4096, 16384], P('tok', 'voc'), may hold values from -320 to 320
- token_ids: int32 [4096], P('tok'), may hold values from 0 to 16383
Outputs:
- loss: float32 [], replicated
- grad_hidden: float32 [4096, 1024], P('tok', 'voc')
- grad_head: float32 [1024, 16384], P('tok', 'voc')
All inputs are finite; a program needn't handle non-finite values.
Results may differ from a plain program's by a relative error of at most 0.015.
Values may be sent and summed in bfloat16 or wider, within the bound.
No kernel may reach another device: no remote copies, remote signals or barrier semaphores. Data moves between devices by JAX's collectives and lax.ppermute only.
A program may use at most 128 MiB of HBM per device.

v0:
```python
import jax
import jax.numpy as jnp
from jax import lax
from jax.sharding import PartitionSpec as P

ce_weight = 0.5


def body(hidden, head_weight, target_logits, token_ids):
    rows = hidden.shape[0]
    share = head_weight.shape[1]
    vocab_start = lax.axis_index("voc") * share
    whole = lax.all_gather(head_weight, "tok", axis=0, tiled=True)
    draft = jnp.dot(hidden, whole, preferred_element_type=jnp.float32)
    target = target_logits.astype(jnp.float32)
    target_max, draft_max = lax.pmax((jnp.max(target, axis=1), jnp.max(draft, axis=1)), "voc")
    target_exp = jnp.exp(target - target_max[:, None])
    draft_exp = jnp.exp(draft - draft_max[:, None])
    target_sum, draft_sum = lax.psum(
        (jnp.sum(target_exp, axis=1), jnp.sum(draft_exp, axis=1)), "voc"
    )
    probs_p = target_exp / target_sum[:, None]
    probs_q = draft_exp / draft_sum[:, None]
    lse_t = target_max + jnp.log(target_sum)
    lse_z = draft_max + jnp.log(draft_sum)
    column = lax.broadcasted_iota(jnp.int32, (rows, share), 1) + vocab_start
    own = (column == token_ids[:, None]).astype(jnp.float32)
    voc_count = lax.axis_size("voc")
    per_token = jnp.sum(probs_p * (target - draft) - ce_weight * own * draft, axis=1)
    per_token = per_token + ((1.0 + ce_weight) * lse_z - lse_t) / voc_count
    total = lax.psum(jnp.sum(per_token), ("tok", "voc"))
    loss = total / (rows * lax.axis_size("tok"))
    slope = ((1.0 + ce_weight) * probs_q - probs_p - ce_weight * own).astype(jnp.bfloat16)
    partial_grad = lax.dot_general(
        slope, whole, (((1,), (1,)), ((), ())), preferred_element_type=jnp.float32
    )
    grad_hidden = lax.psum_scatter(
        partial_grad.astype(jnp.bfloat16), "voc", scatter_dimension=1, tiled=True
    ).astype(jnp.float32)
    grad_head = lax.psum_scatter(
        lax.dot_general(
            hidden, slope, (((0,), (0,)), ((), ())), preferred_element_type=jnp.float32
        ).astype(jnp.bfloat16),
        "tok",
        scatter_dimension=0,
        tiled=True,
    ).astype(jnp.float32)
    return (loss, grad_hidden, grad_head)


def solution(mesh):
    placed = (P("tok", None), P("tok", "voc"), P("tok", "voc"), P("tok"))
    return jax.shard_map(
        body,
        mesh=mesh,
        in_specs=placed,
        out_specs=(P(), P("tok", "voc"), P("tok", "voc")),
        check_vma=False,
    )
```

profile of v0, /device:TPU:0, one launch (start us, length us, event | category | flops | bytes accessed | tf_op | source)
XLA Modules:
  0.0 290.3 jit_solution(11293099033932415413)
XLA Ops:
  7.2 0.0 copy-start
  7.2 0.0 all-gather.2.cloned.1.call-start
  7.2 0.7 all-gather.2.cloned.1.call-update
  7.9 0.0 reduce-scatter.5.cloned.1.call-start
  8.0 2.8 reduce_max.23
  10.8 0.0 copy-start.2
  10.8 83.6 %all-gather.2.cloned.1.call-done = bf16[1024,4096]{1,0:T(8,128)(2,1)} async-done(((bf16[128,4096]{1,0:T(8,128)(2,1)}), bf16[1024,4096]{1,0:T(8,128)(2,1)}) %all-gather.2.cloned.1.call-update) | async-done | bytes 8388624 | tf_op jit(solution)/shard_map/all_gather | solution.py:13
  94.4 0.0 copy-done
  94.4 10.1 %fusion.8 = (f32[512]{0:T(512)S(1)}, f32[512,4096]{1,0:T(8,128)}) fusion(bf16[512,1024]{1,0:T(8,128)(2,1)S(1)} %copy-done, bf16[1024,4096]{1,0:T(8,128)(2,1)} %all-gather.2.cloned.1.call-done), kind=kOutput, calls=%fused_computation.17 | convolution fusion | flops 4297063936 | bytes 17827840 | tf_op jit(solution)/shard_map/dot_general | solution.py:14
  104.5 9.8 %all-reduce = (f32[512]{0:T(512)S(1)}, f32[512]{0:T(512)S(1)}) all-reduce(f32[512]{0:T(512)S(1)} %get-tuple-element.13, bf16[512]{0:T(512)(128)(2,1)S(1)} %reduce_max.23), channel_id=1, replica_groups=mesh['tok'=8,'voc'=4] {'voc'}, use_global_device_ids=true, to_apply=%region_6.0 | all-reduce | flops 1024 | bytes 7168 | tf_op jit(solution)/shard_map/pmax | solution.py:16
  114.3 3.7 %fusion.2 = f32[512]{0:T(512)S(1)} fusion(bf16[512,4096]{1,0:T(8,128)(2,1)} %param.6, f32[512]{0:T(512)S(1)} %get-tuple-element.12), kind=kLoop, calls=%fused_computation.6 | loop fusion | flops 6290944 | bytes 4198400 | tf_op jit(solution)/shard_map/reduce_sum | solution.py:20
  118.0 8.0 %psum.21 = f32[512]{0:T(512)S(1)} all-reduce(f32[512]{0:T(512)S(1)} %fusion.2), channel_id=1, replica_groups=mesh['tok'=8,'voc'=4] {'voc'}, use_global_device_ids=true, to_apply=%region_3.0 | all-reduce | flops 512 | bytes 4096 | tf_op jit(solution)/shard_map/psum | solution.py:19
  126.0 0.0 copy-done.2
  126.0 7.6 %fusion.7 = (f32[512]{0:T(512)S(1)}, f32[512]{0:T(512)S(1)}) fusion(f32[512,4096]{1,0:T(8,128)} %get-tuple-element.14, f32[512]{0:T(512)S(1)} %get-tuple-element.11, s32[512]{0:T(512)S(1)} %copy-done.2, s32[4096]{0:T(1024)S(1)} %iota_add_fusion, f32[512]{0:T(512)S(1)} %psum.21, f32[512]{0:T(512)S(1)} %get-tuple-element.12, bf16[512,4096]{1,0:T(8,128)(2,1)} %param.6), kind=kLoop, calls=%fused_computation.13 | loop fusion | flops 25164800 | bytes 12611584 | tf_op jit(solution)/shard_map/reduce_sum | solution.py:20
  133.6 9.2 %psum.22 = f32[512]{0:T(512)S(1)} all-reduce(f32[512]{0:T(512)S(1)} %get-tuple-element.9), channel_id=1, replica_groups=mesh['tok'=8,'voc'=4] {'voc'}, use_global_device_ids=true, to_apply=%region_8.0 | all-reduce | flops 512 | bytes 4096 | tf_op jit(solution)/shard_map/psum | solution.py:19
  142.7 8.1 %fusion.6 = bf16[512,4096]{1,0:T(8,128)(2,1)S(1)} fusion(f32[512,4096]{1,0:T(8,128)} %get-tuple-element.14, bf16[512,4096]{1,0:T(8,128)(2,1)} %param.6, f32[512]{0:T(512)S(1)} %psum.22, f32[512]{0:T(512)S(1)} %get-tuple-element.11, s32[4096]{0:T(1024)S(1)} %iota_add_fusion, f32[512]{0:T(512)S(1)} %psum.21, f32[512]{0:T(512)S(1)} %get-tuple-element.12, ...), kind=kLoop, calls=%fused_computation.10 | loop fusion | flops 23068672 | bytes 16803840 | tf_op jit(solution)/shard_map/convert_element_type | solution.py:33
  150.8 0.0 copy-start.1
  150.8 2.0 copy-done.1
  152.8 8.0 %convolution_convert_fusion = bf16[512,1024]{1,0:T(8,128)(2,1)} fusion(bf16[512,4096]{1,0:T(8,128)(2,1)S(1)} %fusion.6, bf16[1024,4096]{1,0:T(8,128)(2,1)} %all-gather.2.cloned.1.call-done), kind=kOutput, calls=%fused_computation.14 | convolution fusion | flops 4295491584 | bytes 13631488 | tf_op jit(solution)/shard_map/dot_general | solution.py:34
  160.8 0.0 reduce-scatter.5.cloned.1.call-update
  160.9 0.0 reduce-scatter.7.cloned.1.call-start
  160.9 9.0 %convert_bitcast_fusion = bf16[1024,4096]{0,1:T(8,128)(2,1)} fusion(bf16[512,4096]{1,0:T(8,128)(2,1)} %copy-done.1, bf16[512,1024]{1,0:T(8,128)(2,1)S(1)} %copy-done), kind=kOutput, calls=%fused_computation.11 | convolution fusion | flops 4299161600 | bytes 13631488 | tf_op jit(solution)/shard_map/dot_general | solution.py:41
  169.9 11.3 %copy.9 = bf16[1024,4096]{1,0:T(8,128)(2,1)} copy(bf16[1024,4096]{0,1:T(8,128)(2,1)} %convert_bitcast_fusion) | data formatting | bytes 16777216
  181.3 0.0 reduce-scatter.7.cloned.1.call-update
  181.3 0.6 add_reduce_fusion
  181.9 39.5 %psum.23 = f32[]{:T(128)} all-reduce(f32[]{:T(128)} %add_reduce_fusion), channel_id=1, replica_groups=mesh['tok'=8,'voc'=4] {'tok','voc'}, use_global_device_ids=true, to_apply=%region_10.0 | all-reduce | flops 1 | bytes 8 | tf_op jit(solution)/shard_map/psum | solution.py:31
  222.1 0.0 reduce-scatter.5.cloned.1.call-done
  222.1 1.8 convert_element_type.25
  223.9 55.5 %reduce-scatter.7.cloned.1.call-done = bf16[128,4096]{1,0:T(8,128)(2,1)} async-done(((bf16[1024,4096]{1,0:T(8,128)(2,1)}), bf16[128,4096]{1,0:T(8,128)(2,1)}) %reduce-scatter.7.cloned.1.call-update) | async-done | bytes 1048592
  279.4 1.6 copy.10
  281.0 1.6 copy.8
  (1 shorter events, 0.0 us)
Async XLA Ops:
  7.2 87.2 %copy-start = (bf16[512,1024]{1,0:T(8,128)(2,1)S(1)}, bf16[512,1024]{1,0:T(8,128)(2,1)}, u32[]{:S(2)}) copy-start(bf16[512,1024]{1,0:T(8,128)(2,1)} %param.4) | copy-start | bytes 3145732
  7.2 87.2 %all-gather.2.cloned.1.call-start = ((), (), s32[]{:S(2)}) async-start(), calls=%async_computation.2 | async-start | bytes 9437184 | tf_op jit(solution)/shard_map/all_gather | solution.py:13
  7.9 214.2 %reduce-scatter.5.cloned.1.call-start = ((), (), s32[]{:S(2)}) async-start(), calls=%async_computation.3 | async-start | bytes 1310720 | tf_op jit(solution)/shard_map/reduce_scatter | solution.py:37
  10.8 115.2 %copy-start.2 = (s32[512]{0:T(512)S(1)}, s32[512]{0:T(512)}, u32[]{:S(2)}) copy-start(s32[512]{0:T(512)} %param.7) | copy-start | bytes 6148
  150.8 2.0 copy-start.1
  160.9 118.5 %reduce-scatter.7.cloned.1.call-start = ((), (), s32[]{:S(2)}) async-start(), calls=%async_computation.4 | async-start | bytes 9437184
Sparse Core Ops, SparseCore 0:
  9.6 84.7 all-gather.1
  161.0 25.4 reduce-scatter.4
  188.8 90.5 reduce-scatter.6
where the time goes:
time: 291 us; the launch traced here: 290 us
  waiting for transfers between devices  140 us (48%)
  blocking collectives  66.4 us (23%)
  matrix products  27.2 us (9%)
  other arithmetic  24.6 us (8%)
  local copies, waits for them, and re-layouts  16.5 us (6%)
  between operations  15.6 us (5%)
    all_gather x1, waiting for transfers between devices, body(): whole = lax.all_gather(head_weight, 'tok', axis=0, tiled=True)  83.6 us
    unnamed x4, waiting for transfers between devices  56.3 us
    psum x1, blocking collectives, body(): total = lax.psum(jnp.sum(per_token), ('tok', 'voc'))  39.5 us
    psum x2, blocking collectives, body(): lax.psum((jnp.sum(target_exp, axis=1), jnp.sum(draft_exp, axis=1)), 'voc')  17.1 us
    unnamed x9, local copies, waits for them, and re-layouts  16.5 us
    dot_general x1, matrix products, body(): draft = jnp.dot(hidden, whole, preferred_element_type=jnp.float32)  10.1 us
    pmax x1, blocking collectives, body(): lax.pmax((jnp.max(target, axis=1), jnp.max(draft, axis=1)), 'voc')  9.81 us
    dot_general x1, matrix products, body(): lax.dot_general(hidden, slope, (((0,), (0,)), ((), ())), preferred_elemen...  9.02 us
  transfers between devices with their start and end apart: 3, of which 2 were waited for; matrix products, arithmetic and copies ran while one was open for 9% of the time, Pallas kernels for 0%

commit v1 on v0

--- a/solution.py
+++ b/solution.py
@@ -1,3 +1,4 @@
+import functools
 import jax
 import jax.numpy as jnp
 from jax import lax
@@ -6,11 +7,33 @@
 ce_weight = 0.5
 
 
+def form_widths(content, along_axis):
+    last = jax.lax.axis_size(along_axis)
+    outer = jax.lax.axis_index(along_axis)
+    carry_out, r2, moved = (last, outer, content.shape[0])
+    parts_seen = [idx * carry_out if no == 0 else idx for no, idx in enumerate(content.shape)]
+    z2 = jnp.zeros(parts_seen, content.dtype)
+    formed = lax.dynamic_update_slice_in_dim(z2, content, r2 * moved, axis=0)
+    for jj in tuple(range(1, carry_out)):
+        content = jax.lax.ppermute(
+            content,
+            axis_name=along_axis,
+            perm=[(no, (no + 1) % carry_out) for no in range(carry_out)],
+        )
+        formed = lax.dynamic_update_slice_in_dim(
+            formed, content, (r2 - jj) % carry_out * moved, axis=0
+        )
+    return formed
+
+
+replace_the_sections = functools.partial(form_widths, along_axis="tok")
+
+
 def body(hidden, head_weight, target_logits, token_ids):
     rows = hidden.shape[0]
     share = head_weight.shape[1]
     vocab_start = lax.axis_index("voc") * share
-    whole = lax.all_gather(head_weight, "tok", axis=0, tiled=True)
+    whole = replace_the_sections(head_weight)
     draft = jnp.dot(hidden, whole, preferred_element_type=jnp.float32)
     target = target_logits.astype(jnp.float32)
     target_max, draft_max = lax.pmax((jnp.max(target, axis=1), jnp.max(draft, axis=1)), "voc")

time: 291 us -> 316 us (1.086)
  waiting for transfers between devices: 140 us -> 156 us
  local copies, waits for them, and re-layouts: 16.5 us -> 29.4 us
    ppermute x0 -> x7, waiting for transfers between devices: none -> 99.6 us  [form_widths(): jax.lax.ppermute(content, axis_name=along_axis, perm=[(no, (no + 1) % car...]
    all_gather x1 -> x0, waiting for transfers between devices: 83.6 us -> none  [body(): whole = lax.all_gather(head_weight, 'tok', axis=0, tiled=True)]
    unnamed x9 -> x22, local copies, waits for them, and re-layouts: 16.5 us -> 25 us
    dynamic_update_slice x0 -> x8, local copies, waits for them, and re-layouts: none -> 3.34 us  [the longest x7 3.23 us: form_widths(): lax.dynamic_update_slice_in_dim(formed, content, (r2 - jj) % carry_out *...]
    unnamed x4 -> x3, waiting for transfers between devices: 56.3 us -> 56.1 us
  transfers between devices with their start and end apart: 3 -> 9, of which waited for: 2 -> 8; matrix products, arithmetic and copies ran while one was open for 9% -> 12% of each run, Pallas kernels for 0% -> 0%
where the time goes in v1:
time: 316 us
  waiting for transfers between devices  156 us (49%)
  blocking collectives  66.2 us (21%)
  local copies, waits for them, and re-layouts  29.4 us (9%)
  matrix products  24.5 us (8%)
  other arithmetic  23.1 us (7%)
  between operations  16.1 us (5%)
    ppermute x7, waiting for transfers between devices, form_widths(): jax.lax.ppermute(content, axis_name=along_axis, perm=[(no, (no + 1) % car...  99.6 us
    unnamed x3, waiting for transfers between devices  56.1 us
    psum x1, blocking collectives, body(): total = lax.psum(jnp.sum(per_token), ('tok', 'voc'))  38.7 us
    unnamed x22, local copies, waits for them, and re-layouts  25 us
    psum x2, blocking collectives, body(): lax.psum((jnp.sum(target_exp, axis=1), jnp.sum(draft_exp, axis=1)), 'voc')  17.1 us
    pmax x1, blocking collectives, body(): lax.pmax((jnp.max(target, axis=1), jnp.max(draft, axis=1)), 'voc')  10.4 us
    dot_general x1, matrix products, body(): lax.dot_general(hidden, slope, (((0,), (0,)), ((), ())), preferred_elemen...  8.93 us
    dot_general x1, matrix products, body(): lax.dot_general(slope, whole, (((1,), (1,)), ((), ())), preferred_element...  8.21 us
  transfers between devices with their start and end apart: 9, of which 8 were waited for; matrix products, arithmetic and copies ran while one was open for 12% of the time, Pallas kernels for 0%

profile of v1, /device:TPU:0, one launch (start us, length us, event | category | flops | bytes accessed | tf_op | source)
XLA Modules:
  0.0 315.6 jit_solution(1784160881387144635)
XLA Ops:
  7.2 0.0 copy-start
  7.2 0.0 reduce-scatter.5.cloned.1.call-start
  7.2 0.5 collective-permute-start
  7.8 16.7 %collective-permute-done = bf16[128,4096]{1,0:T(8,128)(2,1)S(1)} collective-permute-done((bf16[128,4096]{1,0:T(8,128)(2,1)}, bf16[128,4096]{1,0:T(8,128)(2,1)S(1)}, u32[]{:S(2)}, u32[]{:S(2)}) %collective-permute-start) | collective-permute-done | bytes 1048608 | tf_op jit(solution)/shard_map/ppermute | solution.py:18
  24.5 0.0 collective-permute-start.1
  24.5 16.0 %collective-permute-done.1 = bf16[128,4096]{1,0:T(8,128)(2,1)S(1)} collective-permute-done((bf16[128,4096]{1,0:T(8,128)(2,1)S(1)}, bf16[128,4096]{1,0:T(8,128)(2,1)S(1)}, u32[]{:S(2)}, u32[]{:S(2)}) %collective-permute-start.1) | collective-permute-done | bytes 1048608 | tf_op jit(solution)/shard_map/ppermute | solution.py:18
  40.5 0.0 copy-start.4
  40.5 1.0 copy-done.4
  41.5 0.0 collective-permute-start.2
  41.5 16.0 %collective-permute-done.2 = bf16[128,4096]{1,0:T(8,128)(2,1)S(1)} collective-permute-done((bf16[128,4096]{1,0:T(8,128)(2,1)S(1)}, bf16[128,4096]{1,0:T(8,128)(2,1)S(1)}, u32[]{:S(2)}, u32[]{:S(2)}) %collective-permute-start.2) | collective-permute-done | bytes 1048608 | tf_op jit(solution)/shard_map/ppermute | solution.py:18
  57.5 0.0 copy-start.6
  57.5 1.0 copy-done.6
  58.5 0.0 collective-permute-start.3
  58.5 16.1 %collective-permute-done.3 = bf16[128,4096]{1,0:T(8,128)(2,1)} collective-permute-done((bf16[128,4096]{1,0:T(8,128)(2,1)S(1)}, bf16[128,4096]{1,0:T(8,128)(2,1)}, u32[]{:S(2)}, u32[]{:S(2)}) %collective-permute-start.3) | collective-permute-done | bytes 1048608 | tf_op jit(solution)/shard_map/ppermute | solution.py:18
  74.6 0.0 collective-permute-start.4
  74.6 6.5 %copy.9 = bf16[512,4096]{0,1:T(8,128)(2,1)} copy(bf16[512,4096]{1,0:T(8,128)(2,1)} %param.6) | data formatting | bytes 8388608 | tf_op args[2]
  81.1 0.0 copy-start.3
  81.1 2.9 reduce_max.23
  84.1 0.0 copy-start.5
  84.1 0.0 copy-start.7
  84.1 1.0 broadcast_in_dim.2
  85.2 0.0 copy-done.3
  85.2 0.1 constant_dynamic-update-slice_fusion.7
  85.3 5.7 %collective-permute-done.4 = bf16[128,4096]{1,0:T(8,128)(2,1)} collective-permute-done((bf16[128,4096]{1,0:T(8,128)(2,1)}, bf16[128,4096]{1,0:T(8,128)(2,1)}, u32[]{:S(2)}, u32[]{:S(2)}) %collective-permute-start.4) | collective-permute-done | bytes 1048608 | tf_op jit(solution)/shard_map/ppermute | solution.py:18
  91.0 0.0 collective-permute-start.5
  91.0 0.1 constant_dynamic-update-slice_fusion.6
  91.1 0.0 copy-done.5
  91.1 0.1 constant_dynamic-update-slice_fusion.5
  91.2 0.0 copy-done.7
  91.2 0.1 constant_dynamic-update-slice_fusion.4
  91.3 15.9 %collective-permute-done.5 = bf16[128,4096]{1,0:T(8,128)(2,1)S(1)} collective-permute-done((bf16[128,4096]{1,0:T(8,128)(2,1)}, bf16[128,4096]{1,0:T(8,128)(2,1)S(1)}, u32[]{:S(2)}, u32[]{:S(2)}) %collective-permute-start.5) | collective-permute-done | bytes 1048608 | tf_op jit(solution)/shard_map/ppermute | solution.py:18
  107.2 0.0 collective-permute-start.6
  107.2 1.3 constant_dynamic-update-slice_fusion.3
  108.5 1.3 constant_dynamic-update-slice_fusion.2
  109.9 0.1 constant_dynamic-update-slice_fusion.1
  110.0 13.2 %collective-permute-done.6 = bf16[128,4096]{1,0:T(8,128)(2,1)S(1)} collective-permute-done((bf16[128,4096]{1,0:T(8,128)(2,1)S(1)}, bf16[128,4096]{1,0:T(8,128)(2,1)S(1)}, u32[]{:S(2)}, u32[]{:S(2)}) %collective-permute-start.6) | collective-permute-done | bytes 1048608 | tf_op jit(solution)/shard_map/ppermute | solution.py:18
  123.2 0.1 constant_dynamic-update-slice_fusion
  123.3 0.0 copy-done
  123.3 0.0 copy-start.1
  123.4 0.0 copy-start.8
  123.4 7.4 %fusion.9 = (f32[512]{0:T(512)S(1)}, f32[4096,512]{1,0:T(8,128)}) fusion(bf16[1024,4096]{1,0:T(8,128)(2,1)S(1)} %constant_dynamic-update-slice_fusion, bf16[512,1024]{1,0:T(8,128)(2,1)S(1)} %copy-done), kind=kOutput, calls=%fused_computation.26 | convolution fusion | flops 4297063936 | bytes 17827840 | tf_op jit(solution)/shard_map/dot_general | solution.py:37
  130.7 0.0 copy-done.1
  130.7 10.4 %all-reduce = (f32[512]{0:T(512)S(1)}, f32[512]{0:T(512)S(1)}) all-reduce(f32[512]{0:T(512)S(1)} %get-tuple-element.13, bf16[512]{0:T(512)(128)(2,1)S(1)} %reduce_max.23), channel_id=1, replica_groups=mesh['tok'=8,'voc'=4] {'voc'}, use_global_device_ids=true, to_apply=%region_6.7 | all-reduce | flops 1024 | bytes 7168 | tf_op jit(solution)/shard_map/pmax | solution.py:39
  141.1 3.6 %fusion.2 = f32[512]{0:T(512)S(1)} fusion(bf16[512,4096]{0,1:T(8,128)(2,1)} %copy.9, f32[512]{0:T(512)S(1)} %get-tuple-element.12), kind=kLoop, calls=%fused_computation.6 | loop fusion | flops 6290944 | bytes 4198400 | tf_op jit(solution)/shard_map/reduce_sum | solution.py:43
  144.8 7.9 %psum.21 = f32[512]{0:T(512)S(1)} all-reduce(f32[512]{0:T(512)S(1)} %fusion.2), channel_id=1, replica_groups=mesh['tok'=8,'voc'=4] {'voc'}, use_global_device_ids=true, to_apply=%region_3.4 | all-reduce | flops 512 | bytes 4096 | tf_op jit(solution)/shard_map/psum | solution.py:42
  152.7 0.0 copy-done.8
  152.7 7.2 %fusion.8 = (f32[512]{0:T(512)S(1)}, f32[512]{0:T(512)S(1)}) fusion(f32[4096,512]{1,0:T(8,128)} %get-tuple-element.14, f32[512]{0:T(512)S(1)} %get-tuple-element.11, s32[512]{0:T(512)S(1)} %copy-done.8, s32[4096]{0:T(1024)S(1)} %iota_add_fusion, f32[512]{0:T(512)S(1)} %psum.21, f32[512]{0:T(512)S(1)} %get-tuple-element.12, bf16[512,4096]{0,1:T(8,128)(2,1)} %copy.9), kind=kLoop, calls=%fused_computation.14 | loop fusion | flops 25164800 | bytes 12611584 | tf_op jit(solution)/shard_map/reduce_sum | solution.py:43
  159.9 9.2 %psum.22 = f32[512]{0:T(512)S(1)} all-reduce(f32[512]{0:T(512)S(1)} %get-tuple-element.9), channel_id=1, replica_groups=mesh['tok'=8,'voc'=4] {'voc'}, use_global_device_ids=true, to_apply=%region_8.9 | all-reduce | flops 512 | bytes 4096 | tf_op jit(solution)/shard_map/psum | solution.py:42
  169.1 6.9 %fusion.6 = bf16[512,4096]{0,1:T(8,128)(2,1)S(1)} fusion(f32[4096,512]{1,0:T(8,128)} %get-tuple-element.14, bf16[512,4096]{0,1:T(8,128)(2,1)} %copy.9, f32[512]{0:T(512)S(1)} %psum.22, f32[512]{0:T(512)S(1)} %get-tuple-element.11, s32[512]{0:T(512)S(1)} %copy-done.8, f32[512]{0:T(512)S(1)} %psum.21, f32[512]{0:T(512)S(1)} %get-tuple-element.12, ...), kind=kLoop, calls=%fused_computation.10 | loop fusion | flops 23068672 | bytes 16803840 | tf_op jit(solution)/shard_map/convert_element_type | solution.py:56
  176.1 0.0 copy-start.2
  176.1 1.9 copy-done.2
  178.0 8.2 %convolution_convert_fusion = bf16[512,1024]{1,0:T(8,128)(2,1)} fusion(bf16[512,4096]{0,1:T(8,128)(2,1)S(1)} %fusion.6, bf16[1024,4096]{1,0:T(8,128)(2,1)} %copy-done.1), kind=kOutput, calls=%fused_computation.15 | convolution fusion | flops 4295491584 | bytes 13631488 | tf_op jit(solution)/shard_map/dot_general | solution.py:57
  186.2 0.0 reduce-scatter.5.cloned.1.call-update
  186.2 0.0 reduce-scatter.7.cloned.1.call-start
  186.3 8.9 %convert_bitcast_fusion = bf16[1024,4096]{0,1:T(8,128)(2,1)} fusion(bf16[512,4096]{0,1:T(8,128)(2,1)} %copy-done.2, bf16[512,1024]{1,0:T(8,128)(2,1)S(1)} %copy-done), kind=kOutput, calls=%fused_computation.13 | convolution fusion | flops 4299161600 | bytes 13631488 | tf_op jit(solution)/shard_map/dot_general | solution.py:64
  195.2 11.3 %copy.11 = bf16[1024,4096]{1,0:T(8,128)(2,1)} copy(bf16[1024,4096]{0,1:T(8,128)(2,1)} %convert_bitcast_fusion) | data formatting | bytes 16777216
  206.5 0.0 reduce-scatter.7.cloned.1.call-update
  206.6 0.6 add_reduce_fusion
  207.2 38.7 %psum.23 = f32[]{:T(128)} all-reduce(f32[]{:T(128)} %add_reduce_fusion), channel_id=1, replica_groups=mesh['tok'=8,'voc'=4] {'tok','voc'}, use_global_device_ids=true, to_apply=%region_10.11 | all-reduce | flops 1 | bytes 8 | tf_op jit(solution)/shard_map/psum | solution.py:54
  246.5 0.0 reduce-scatter.5.cloned.1.call-done
  246.5 1.8 convert_element_type.25
  248.3 56.1 %reduce-scatter.7.cloned.1.call-done = bf16[128,4096]{1,0:T(8,128)(2,1)} async-done(((bf16[1024,4096]{1,0:T(8,128)(2,1)}), bf16[128,4096]{1,0:T(8,128)(2,1)}) %reduce-scatter.7.cloned.1.call-update) | async-done | bytes 1048592
  304.4 1.6 copy.12
  306.0 1.6 copy.10
  (1 shorter events, 0.0 us)
Async XLA Ops:
  7.2 116.2 %copy-start = (bf16[512,1024]{1,0:T(8,128)(2,1)S(1)}, bf16[512,1024]{1,0:T(8,128)(2,1)}, u32[]{:S(2)}) copy-start(bf16[512,1024]{1,0:T(8,128)(2,1)} %param.4) | copy-start | bytes 3145732
  7.2 239.3 %reduce-scatter.5.cloned.1.call-start = ((), (), s32[]{:S(2)}) async-start(), calls=%async_computation.2 | async-start | bytes 1310720 | tf_op jit(solution)/shard_map/reduce_scatter | solution.py:60
  7.2 17.3 %collective-permute-start = (bf16[128,4096]{1,0:T(8,128)(2,1)}, bf16[128,4096]{1,0:T(8,128)(2,1)S(1)}, u32[]{:S(2)}, u32[]{:S(2)}) collective-permute-start(bf16[128,4096]{1,0:T(8,128)(2,1)} %param.5), channel_id=1, source_target_pairs={{0,4},{4,8},{8,12},{12,16},{16,20},{20,24},{24,28},{28,0},{1,5},{5... | collective-permute-start | bytes 3145736 | tf_op jit(solution)/shard_map/ppermute | solution.py:18
  24.5 16.0 %collective-permute-start.1 = (bf16[128,4096]{1,0:T(8,128)(2,1)S(1)}, bf16[128,4096]{1,0:T(8,128)(2,1)S(1)}, u32[]{:S(2)}, u32[]{:S(2)}) collective-permute-start(bf16[128,4096]{1,0:T(8,128)(2,1)S(1)} %collective-permute-done), channel_id=1, source_target_pairs={{0,4},{4,8},{8,12},{12,16},{16,20},{20,24},{24,28},{28,0},{1,5},{5... | collective-permute-start | bytes 3145736 | tf_op jit(solution)/shard_map/ppermute | solution.py:18
  40.5 1.0 copy-start.4
  41.5 16.0 %collective-permute-start.2 = (bf16[128,4096]{1,0:T(8,128)(2,1)S(1)}, bf16[128,4096]{1,0:T(8,128)(2,1)S(1)}, u32[]{:S(2)}, u32[]{:S(2)}) collective-permute-start(bf16[128,4096]{1,0:T(8,128)(2,1)S(1)} %collective-permute-done.1), channel_id=1, source_target_pairs={{0,4},{4,8},{8,12},{12,16},{16,20},{20,24},{24,28},{28,0},{1,5},{5... | collective-permute-start | bytes 3145736 | tf_op jit(solution)/shard_map/ppermute | solution.py:18
  57.5 1.0 copy-start.6
  58.5 16.1 %collective-permute-start.3 = (bf16[128,4096]{1,0:T(8,128)(2,1)S(1)}, bf16[128,4096]{1,0:T(8,128)(2,1)}, u32[]{:S(2)}, u32[]{:S(2)}) collective-permute-start(bf16[128,4096]{1,0:T(8,128)(2,1)S(1)} %collective-permute-done.2), channel_id=1, source_target_pairs={{0,4},{4,8},{8,12},{12,16},{16,20},{20,24},{24,28},{28,0},{1,5},{5... | collective-permute-start | bytes 3145736 | tf_op jit(solution)/shard_map/ppermute | solution.py:18
  74.6 16.3 %collective-permute-start.4 = (bf16[128,4096]{1,0:T(8,128)(2,1)}, bf16[128,4096]{1,0:T(8,128)(2,1)}, u32[]{:S(2)}, u32[]{:S(2)}) collective-permute-start(bf16[128,4096]{1,0:T(8,128)(2,1)} %collective-permute-done.3), channel_id=1, source_target_pairs={{0,4},{4,8},{8,12},{12,16},{16,20},{20,24},{24,28},{28,0},{1,5},{5... | collective-permute-start | bytes 3145736 | tf_op jit(solution)/shard_map/ppermute | solution.py:18
  81.1 4.0 %copy-start.3 = (bf16[128,4096]{1,0:T(8,128)(2,1)S(1)}, bf16[128,4096]{1,0:T(8,128)(2,1)}, u32[]{:S(2)}) copy-start(bf16[128,4096]{1,0:T(8,128)(2,1)} %param.5) | copy-start | bytes 3145732
  84.1 7.0 %copy-start.5 = (bf16[128,4096]{1,0:T(8,128)(2,1)S(1)}, bf16[128,4096]{1,0:T(8,128)(2,1)}, u32[]{:S(2)}) copy-start(bf16[128,4096]{1,0:T(8,128)(2,1)} %copy-done.4) | copy-start | bytes 3145732
  84.1 7.1 %copy-start.7 = (bf16[128,4096]{1,0:T(8,128)(2,1)S(1)}, bf16[128,4096]{1,0:T(8,128)(2,1)}, u32[]{:S(2)}) copy-start(bf16[128,4096]{1,0:T(8,128)(2,1)} %copy-done.6) | copy-start | bytes 3145732
  91.0 16.2 %collective-permute-start.5 = (bf16[128,4096]{1,0:T(8,128)(2,1)}, bf16[128,4096]{1,0:T(8,128)(2,1)S(1)}, u32[]{:S(2)}, u32[]{:S(2)}) collective-permute-start(bf16[128,4096]{1,0:T(8,128)(2,1)} %collective-permute-done.4), channel_id=1, source_target_pairs={{0,4},{4,8},{8,12},{12,16},{16,20},{20,24},{24,28},{28,0},{1,5},{5... | collective-permute-start | bytes 3145736 | tf_op jit(solution)/shard_map/ppermute | solution.py:18
  107.2 16.0 %collective-permute-start.6 = (bf16[128,4096]{1,0:T(8,128)(2,1)S(1)}, bf16[128,4096]{1,0:T(8,128)(2,1)S(1)}, u32[]{:S(2)}, u32[]{:S(2)}) collective-permute-start(bf16[128,4096]{1,0:T(8,128)(2,1)S(1)} %collective-permute-done.5), channel_id=1, source_target_pairs={{0,4},{4,8},{8,12},{12,16},{16,20},{20,24},{24,28},{28,0},{1,5},{5... | collective-permute-start | bytes 3145736 | tf_op jit(solution)/shard_map/ppermute | solution.py:18
  123.3 7.4 %copy-start.1 = (bf16[1024,4096]{1,0:T(8,128)(2,1)}, bf16[1024,4096]{1,0:T(8,128)(2,1)S(1)}, u32[]{:S(2)}) copy-start(bf16[1024,4096]{1,0:T(8,128)(2,1)S(1)} %constant_dynamic-update-slice_fusion) | copy-start | bytes 25165828
  123.4 29.3 %copy-start.8 = (s32[512]{0:T(512)S(1)}, s32[512]{0:T(512)}, u32[]{:S(2)}) copy-start(s32[512]{0:T(512)} %param.7) | copy-start | bytes 6148
  176.1 1.9 copy-start.2
  186.2 118.2 %reduce-scatter.7.cloned.1.call-start = ((), (), s32[]{:S(2)}) async-start(), calls=%async_computation.3 | async-start | bytes 9437184
Sparse Core Ops, SparseCore 0:
  186.4 25.0 reduce-scatter.4
  213.8 90.5 reduce-scatter.6
